TPU v7x, 32 devices: a whole 2x2x4 slice. The times are simulated.
32 devices in a mesh: expert: 4 (over x, core), shard: 8 (over z, y).
Axes of the slice: x: 2, y: 2, z: 4, core: 2. Of those that a mesh axis runs over, the one named last changes fastest.
Arguments:
- tokens_in: bfloat16 [1024, 4096], P(('expert', 'shard')), may hold values from -6 to 6
- out_grad: bfloat16 [1024, 2, 8192], P(('expert', 'shard')), may hold values from -6 to 6
- expert_ids: int32 [1024, 2], P(('expert', 'shard')), may hold values from 0 to 3, all different within a row; in each aligned block of 32 rows (0 to 31, 32 to 63, ...) at most 20 rows name the same one
- d_levels: int32 [4, 16], P('expert'), may hold values from 0 to 7
- f_levels: int32 [4, 32], P('expert', 'shard'), may hold values from 0 to 7
Outputs:
- ascent: bfloat16 [4, 4096, 8192], P('expert', None, 'shard')
Inputs may be any that keep to these rules, and one draw needn't show every extreme that they name: `expert_ids`: each token names two different experts; among the 64 entries of one device no expert is named more than 20 times, and 20 is reached on some device; every expert is named somewhere.
All inputs are finite; a program needn't handle non-finite values.
Results may differ from a plain program's by a relative error of at most 0.001.
Values may be sent and summed in bfloat16 or wider, within the bound.
A program may use at most 128 MiB of HBM per device.

v0:
```python
import jax
import jax.numpy as jnp
from jax import lax
from jax.sharding import PartitionSpec as P

BLK = 256


def invert_blocks(blocks):
    lower = jnp.linalg.cholesky(blocks)
    identity = jnp.eye(blocks.shape[-1], dtype=blocks.dtype)
    return jax.vmap(lambda factor: jax.scipy.linalg.cho_solve((factor, True), identity))(lower)


def damping(levels):
    return 0.05 * jnp.exp(0.4 * levels.astype(jnp.float32))


def covariance(rows, levels, row_count):
    blocks = rows.reshape(rows.shape[0], -1, BLK)
    cov = jnp.einsum("rbi,rbj->bij", blocks, blocks, preferred_element_type=jnp.float32) / row_count
    return cov + damping(levels)[:, None, None] * jnp.eye(BLK, dtype=jnp.float32)


def local(tokens_in, out_grad, expert_ids, d_levels, f_levels):
    group_count = lax.axis_size("expert")
    shard_count = lax.axis_size("shard")
    tok_rows = tokens_in.shape[0]
    width = tokens_in.shape[1]
    ff_full = out_grad.shape[2]
    ff_dev = ff_full // shard_count
    capacity = min(tok_rows, max(2, 5 * tok_rows // (2 * group_count)))
    slot_total = group_count * capacity
    flat_ids = expert_ids.reshape(-1)
    member = (flat_ids[:, None] == jnp.arange(group_count, dtype=jnp.int32)[None, :]).astype(
        jnp.int32
    )
    before = jnp.cumsum(member, axis=0) - member
    ranking = jnp.sum(before * member, axis=1)
    target = flat_ids * capacity + ranking
    dispatch = (jnp.arange(slot_total, dtype=jnp.int32)[:, None] == target[None, :]).astype(
        jnp.bfloat16
    )
    per_token = jnp.sum(
        dispatch.reshape(slot_total, tok_rows, 2).astype(jnp.float32), axis=2
    ).astype(jnp.bfloat16)
    x_send = jnp.dot(per_token, tokens_in, preferred_element_type=jnp.float32).astype(jnp.bfloat16)
    g_send = jnp.dot(
        dispatch, out_grad.reshape(2 * tok_rows, ff_full), preferred_element_type=jnp.float32
    ).astype(jnp.bfloat16)
    valid_slot = jnp.sum(dispatch.astype(jnp.float32), axis=1).astype(jnp.bfloat16)
    x_group, g_group, v_group = (
        lax.all_to_all(
            x_send.reshape(group_count, capacity, width),
            "expert",
            split_axis=0,
            concat_axis=1,
            tiled=True,
        ),
        lax.all_to_all(
            g_send.reshape(group_count, capacity, ff_full),
            "expert",
            split_axis=0,
            concat_axis=1,
            tiled=True,
        ),
        lax.all_to_all(
            valid_slot.reshape(group_count, capacity),
            "expert",
            split_axis=0,
            concat_axis=1,
            tiled=True,
        ),
    )
    rows_x, live_rows = (
        lax.all_gather(x_group, "shard", axis=1, tiled=True),
        lax.all_gather(v_group, "shard", axis=1, tiled=True),
    )
    rows_g = lax.all_to_all(g_group, "shard", split_axis=2, concat_axis=1, tiled=True)
    rows_x = rows_x.reshape(-1, width)
    rows_g = rows_g.reshape(-1, ff_dev)
    row_count = jnp.sum(live_rows.astype(jnp.float32))
    gradient = lax.dot_general(
        rows_x, rows_g, (((0,), (0,)), ((), ())), preferred_element_type=jnp.float32
    )
    inv_f = invert_blocks(covariance(rows_g, f_levels[0], row_count))
    grad_blocks = gradient.reshape(width // BLK, BLK, ff_dev)
    highest = lax.Precision.HIGHEST
    own_blocks = width // BLK // shard_count
    first_block = lax.axis_index("shard") * own_blocks
    own_rows = lax.dynamic_slice_in_dim(rows_x, first_block * BLK, own_blocks * BLK, 1)
    own_levels = lax.dynamic_slice_in_dim(d_levels[0], first_block, own_blocks, 0)
    inv_a = invert_blocks(covariance(own_rows, own_levels, row_count))
    left_done = jnp.einsum(
        "bij,bjf->bif",
        lax.all_gather(inv_a, "shard", axis=0, tiled=True),
        grad_blocks,
        precision=highest,
    )
    precond = jnp.einsum(
        "dcj,cjk->dck", left_done.reshape(width, ff_dev // BLK, BLK), inv_f, precision=highest
    ).reshape(width, ff_dev)
    norm_total = lax.psum(jnp.sum(precond * precond), ("expert", "shard"))
    ascent_scale = lax.rsqrt(norm_total / (group_count * width * ff_full) + 1e-06)
    return (precond * ascent_scale).astype(jnp.bfloat16)[None]


def solution(mesh):
    return jax.shard_map(
        local,
        mesh=mesh,
        in_specs=(
            P(("expert", "shard"), None),
            P(("expert", "shard"), None, None),
            P(("expert", "shard"), None),
            P("expert", None),
            P("expert", "shard"),
        ),
        out_specs=P("expert", None, "shard"),
        check_vma=False,
    )
```

profile of v0, /device:TPU:0, one launch (start us, length us, event | category | flops | bytes accessed | tf_op | source)
XLA Modules:
  0.0 676.1 jit_solution(11534804795812444572)
XLA Ops:
  9.3 15.7 %all_to_all.56 = bf16[4,20,4096]{2,1,0:T(8,128)(2,1)S(1)} all-to-all(bf16[4,20,4096]{2,1,0:T(8,128)(2,1)S(1)} %reshape.180), channel_id=1, replica_groups=mesh['expert'=4,'shard'=8] {'expert'}, dimensions={0} | all-to-all | bytes 1310720 | tf_op jit(solution)/shard_map/all_to_all | solution.py:53
  41.6 22.1 %all-reduce.2 = bf16[640]{0:T(1024)(128)(2,1)S(1)} all-reduce(bf16[640]{0:T(1024)(128)(2,1)S(1)} %dynamic-update-slice.22), channel_id=1, replica_groups=mesh['expert'=4,'shard'=8] {'shard'}, use_global_device_ids=true, to_apply=%add.2 | all-reduce | flops 640 | bytes 2560
  64.8 6.8 %copy.134 = bf16[1,80,8192]{1,0,2:T(2,128)(2,1)} copy(bf16[1,80,8192]{2,1,0:T(8,128)(2,1)S(1)} %all_to_all.42) | data formatting | bytes 2621440 | tf_op jit(solution)/shard_map/all_to_all | solution.py:60
  72.1 45.2 %reduce.30 = bf16[8192,80]{1,0:T(8,128)(2,1)S(1)} reduce(bf16[8192,1,80]{2,1,0:T(2,128)(2,1)} %bitcast.114, bf16[]{:T(256)} %broadcast.357), dimensions={1}, to_apply=%bitcast.71.reduce_sub_computation | reduce | bytes 2621442
  129.2 23.5 %custom-call.44 = f32[2,128,128]{2,1,0:T(8,128)S(1)} custom-call(f32[2,128,128]{2,1,0:T(8,128)S(1)} %cholesky.241), custom_call_target="Cholesky" | custom-call | tf_op jit(solution)/shard_map/jit(cholesky)/cholesky | solution.py:10
  153.4 19.7 %custom-call.45 = f32[2,1,128,128]{2,3,1,0:T(8,128)S(1)} custom-call(f32[2,1,128,128]{3,2,1,0:T(8,128)S(1)} %select_bitcast_fusion.1), custom_call_target="InvertDiagBlocksLowerTriangular" | custom-call | tf_op jit(solution)/shard_map/jit(cholesky)/cholesky | solution.py:10
  173.8 23.5 %custom-call.46 = f32[2,128,128]{2,1,0:T(8,128)S(1)} custom-call(f32[2,128,128]{2,1,0:T(8,128)S(1)} %convolution_subtract_fusion.5), custom_call_target="Cholesky" | custom-call | tf_op jit(solution)/shard_map/jit(cholesky)/cholesky | solution.py:10
  199.2 5.3 while.3
  204.5 40.3 %custom-call.47 = f32[2,2,128,128]{2,3,1,0:T(8,128)S(1)} custom-call(f32[2,2,128,128]{3,2,1,0:T(8,128)} %bitcast.125), custom_call_target="InvertDiagBlocksLowerTriangular" | custom-call | tf_op jit(solution)/shard_map/vmap(jit(_cho_solve))/triangular_solve | solution.py:12
  249.1 5.7 reshape.237
  254.8 8.3 %copy.135 = bf16[1,80,8192]{2,1,0:T(8,128)(2,1)S(1)} copy(bf16[1,80,8192]{1,0,2:T(2,128)(2,1)} %bitcast.115) | data formatting | bytes 2621440 | tf_op jit(solution)/shard_map/all_to_all | solution.py:79
  273.5 47.3 %custom-call.40 = f32[4,128,128]{2,1,0:T(8,128)S(1)} custom-call(f32[4,128,128]{2,1,0:T(8,128)S(1)} %cholesky.238), custom_call_target="Cholesky" | custom-call | tf_op jit(solution)/shard_map/jit(cholesky)/cholesky | solution.py:10
  321.0 39.9 %custom-call.41 = f32[4,1,128,128]{2,3,1,0:T(8,128)} custom-call(f32[4,1,128,128]{3,2,1,0:T(8,128)S(1)} %select_bitcast_fusion), custom_call_target="InvertDiagBlocksLowerTriangular" | custom-call | tf_op jit(solution)/shard_map/jit(cholesky)/cholesky | solution.py:10
  364.7 47.7 %custom-call.42 = f32[4,128,128]{2,1,0:T(8,128)S(1)} custom-call(f32[4,128,128]{2,1,0:T(8,128)} %convolution_subtract_fusion.4), custom_call_target="Cholesky" | custom-call | tf_op jit(solution)/shard_map/jit(cholesky)/cholesky | solution.py:10
  414.9 5.3 while.2
  420.2 79.6 %custom-call.43 = f32[4,2,128,128]{2,3,1,0:T(8,128)S(1)} custom-call(f32[4,2,128,128]{3,2,1,0:T(8,128)} %bitcast.124), custom_call_target="InvertDiagBlocksLowerTriangular" | custom-call | tf_op jit(solution)/shard_map/vmap(jit(_cho_solve))/triangular_solve | solution.py:12
  505.4 7.8 %copy.157 = bf16[4096,640]{1,0:T(8,128)(2,1)} copy(bf16[4096,640]{0,1:T(8,128)(2,1)} %bitcast.116) | data formatting | bytes 10485760 | tf_op jit(solution)/shard_map/dot_general | solution.py:83
  513.3 12.7 %fusion.41 = f32[16,256,1024]{2,1,0:T(8,128)} fusion(bf16[16,256,640]{2,1,0:T(8,128)(2,1)} %bitcast.117, bf16[640,1024,1]{1,0,2:T(8,128)(2,1)S(1)} %bitcast.118), kind=kOutput, calls=%fused_computation.98 | convolution fusion | flops 5368709120 | bytes 23330816 | tf_op jit(solution)/shard_map/dot_general | solution.py:83
  525.9 22.9 %fusion.42 = f32[16,256,1024]{2,1,0:T(8,128)} fusion(f32[16,256,256]{2,1,0:T(8,128)} %all-gather.5.cloned.1.call-done, f32[16,256,1024]{2,1,0:T(8,128)} %fusion.41), kind=kOutput, calls=%fused_computation.99 | convolution fusion | flops 12884901888 | bytes 37748736 | tf_op jit(solution)/shard_map/bij,bjf->bif/dot_general | solution.py:94
  548.8 20.4 %reshape.184 = f32[4096,4,256]{2,1,0:T(4,128)} reshape(f32[16,256,1024]{2,1,0:T(8,128)} %fusion.42) | data formatting | bytes 33554432 | tf_op jit(solution)/shard_map/reshape | solution.py:101
  569.2 36.8 %multiply_reduce_fusion = (f32[]{:T(128)}, f32[4,256,4096]{2,1,0:T(8,128)}) fusion(f32[4096,4,256]{2,1,0:T(4,128)} %reshape.184, f32[4,128,256]{2,1,0:T(8,128)S(1)} %fusion.14, f32[4,128,256]{2,1,0:T(8,128)S(1)} %fusion.13), kind=kOutput, calls=%fused_computation.7 | convolution fusion | flops 12893552640 | bytes 34603012 | tf_op jit(solution)/shard_map/dcj,cjk->dck/dot_general | solution.py:100
  606.0 41.1 %psum.7 = f32[]{:T(128)} all-reduce(f32[]{:T(128)} %get-tuple-element.53), channel_id=1, replica_groups=mesh['expert'=4,'shard'=8] {'expert','shard'}, use_global_device_ids=true, to_apply=%region_14.15 | all-reduce | flops 1 | bytes 8 | tf_op jit(solution)/shard_map/psum | solution.py:103
  647.8 9.1 %multiply_convert_fusion = bf16[4,256,4096]{2,1,0:T(8,128)(2,1)} fusion(f32[4,256,4096]{2,1,0:T(8,128)} %get-tuple-element.54, f32[]{:T(128)S(6)} %rsqrt.3), kind=kLoop, calls=%fused_computation.6 | loop fusion | flops 8388608 | bytes 25165828 | tf_op jit(solution)/shard_map/convert_element_type | solution.py:105
  656.9 12.0 %copy.161 = bf16[1,4096,1024]{2,1,0:T(8,128)(2,1)} copy(bf16[1,4096,1024]{1,2,0:T(8,128)(2,1)} %bitcast.113) | data formatting | bytes 16777216 | tf_op jit(solution)/shard_map/convert_element_type | solution.py:105
  (129 shorter events, 72.4 us)
Async XLA Ops:
  6.5 2.2 copy-start
  6.5 119.2 %all-gather.3.cloned.1.call-start = ((), (), s32[]{:S(2)}) async-start(), calls=%async_computation.4 | async-start | bytes 5898240 | tf_op jit(solution)/shard_map/all_gather | solution.py:76
  25.9 7.4 %copy-start.10 = (u32[32]{0:T(128)S(1)}, u32[32]{0:T(128)}, u32[]{:S(2)}) copy-start(u32[32]{0:T(128)} %constant.263) | copy-start | bytes 388
  26.8 7.9 %all-to-all-start.2 = ((bf16[4,1,20]{2,1,0:T(2,128)(2,1)}), bf16[4,1,20]{2,1,0:T(2,128)(2,1)S(1)}, u32[]{:S(2)}, u32[]{:S(2)}) async-start(bf16[4,1,20]{2,1,0:T(2,128)(2,1)} %all_to_all.51), calls=%async_computation.2 | async-start | bytes 4096 | tf_op jit(solution)/shard_map/all_to_all | solution.py:67
  31.4 7.3 %copy-start.8 = (s32[1,16]{1,0:T(1,128)S(1)}, s32[1,16]{1,0:T(1,128)}, u32[]{:S(2)}) copy-start(s32[1,16]{1,0:T(1,128)} %param.8) | copy-start | bytes 196
  34.7 29.8 %all-to-all-start = ((bf16[4,20,8192]{2,1,0:T(8,128)(2,1)}), bf16[4,20,8192]{2,1,0:T(8,128)(2,1)S(1)}, u32[]{:S(2)}, u32[]{:S(2)}) async-start(bf16[4,20,8192]{2,1,0:T(8,128)(2,1)} %reshape.179), calls=%async_computation | async-start | bytes 3145728 | tf_op jit(solution)/shard_map/all_to_all | solution.py:60
  121.9 127.1 %all-to-all-start.1 = ((bf16[8,2,40960]{2,1,0:T(2,128)(2,1)}), bf16[8,2,40960]{2,1,0:T(2,128)(2,1)S(1)}, u32[]{:S(2)}, u32[]{:S(2)}) async-start(bf16[8,2,40960]{2,1,0:T(2,128)(2,1)} %reshape.236), calls=%async_computation.1 | async-start | bytes 2621440 | tf_op jit(solution)/shard_map/all_to_all | solution.py:79
  125.5 400.4 %all-gather.5.cloned.1.call-start = ((), (), s32[]{:S(2)}) async-start(), calls=%async_computation.5 | async-start | bytes 4718592 | tf_op jit(solution)/shard_map/all_gather | solution.py:96
  197.6 51.5 %copy-start.9 = (s32[1,4]{1,0:T(1,128)S(1)}, s32[1,4]{1,0:T(1,128)}, u32[]{:S(2)}) copy-start(s32[1,4]{1,0:T(1,128)} %param.9) | copy-start | bytes 52
  269.7 51.2 %copy-start.7 = (pred[128,128]{1,0:T(8,128)(4,1)S(1)}, pred[128,128]{1,0:T(8,128)(4,1)}, u32[]{:S(2)}) copy-start(pred[128,128]{1,0:T(8,128)(4,1)} %iota_compare_fusion.3) | copy-start | bytes 49156
  271.0 142.4 %copy-start.6 = (pred[256,256]{1,0:T(8,128)(4,1)S(1)}, pred[256,256]{1,0:T(8,128)(4,1)}, u32[]{:S(2)}) copy-start(pred[256,256]{1,0:T(8,128)(4,1)} %iota_compare_fusion.2) | copy-start | bytes 196612
  272.5 1.0 copy-start.3
  360.9 139.5 %copy-start.5 = (f32[128,256]{1,0:T(8,128)S(1)}, f32[128,256]{1,0:T(8,128)}, u32[]{:S(2)}) copy-start(f32[128,256]{1,0:T(8,128)} %get-tuple-element.46) | copy-start | bytes 393220
  412.5 1.0 copy-start.2
  499.8 1.2 copy-start.4
  656.9 12.0 %copy-start.1 = (bf16[32,4096]{1,0:T(8,128)(2,1)S(1)}, bf16[32,4096]{1,0:T(8,128)(2,1)}, u32[]{:S(2)}) copy-start(bf16[32,4096]{1,0:T(8,128)(2,1)} %param.5) | copy-start | bytes 786436
Sparse Core Ops, SparseCore 0:
  26.1 86.4 all-gather.2
  249.1 74.5 all-gather.4
where the time goes:
time: 685 us; the launch traced here: 676 us
  other arithmetic  387 us (56%)
  local copies, waits for them, and re-layouts  93.3 us (14%)
  matrix products  90.7 us (13%)
  blocking collectives  79 us (12%)
  between operations  15.7 us (2%)
  starting transfers between devices  10.5 us (2%)
    another operation x18, other arithmetic, invert_blocks(): lower = jnp.linalg.cholesky(blocks)  203 us
    another operation x7, other arithmetic, invert_blocks(): jax.scipy.linalg.cho_solve((factor, True), identity)  124 us
    unnamed x3, other arithmetic  45.2 us
    psum x1, blocking collectives, local(): norm_total = lax.psum(jnp.sum(precond * precond), ('expert', 'shard'))  41.1 us
    dot_general x1, matrix products, local(): jnp.einsum('dcj,cjk->dck', left_done.reshape(width, ff_dev // BLK, BLK),...  36.8 us
    dot_general x1, matrix products, local(): jnp.einsum('bij,bjf->bif', lax.all_gather(inv_a, 'shard', axis=0, tiled=T...  22.9 us
    unnamed x1, blocking collectives  22.1 us
    reshape x1, local copies, waits for them, and re-layouts, local(): left_done.reshape(width, ff_dev // BLK, BLK)  20.4 us
  transfers between devices with their start and end apart: 5, of which 0 were waited for; matrix products, arithmetic and copies ran while one was open for 69% of the time, Pallas kernels for 0%

commit v1 on v0

--- a/solution.py
+++ b/solution.py
@@ -4,6 +4,12 @@
 from jax.sharding import PartitionSpec as P
 
 BLK = 256
+
+
+def resolve_the_core(local_array, axis_name, axis_no, axis_k):
+    now = jnp.stack(jnp.split(local_array, lax.axis_size(axis_name), axis=axis_no), axis=0)
+    prior = lax.all_to_all(now, axis_name, 0, 0)
+    return jnp.concatenate(prior, axis=axis_k)
 
 
 def invert_blocks(blocks):
@@ -50,12 +56,8 @@
     ).astype(jnp.bfloat16)
     valid_slot = jnp.sum(dispatch.astype(jnp.float32), axis=1).astype(jnp.bfloat16)
     x_group, g_group, v_group = (
-        lax.all_to_all(
-            x_send.reshape(group_count, capacity, width),
-            "expert",
-            split_axis=0,
-            concat_axis=1,
-            tiled=True,
+        resolve_the_core(
+            x_send.reshape(group_count, capacity, width), axis_name="expert", axis_no=0, axis_k=1
         ),
         lax.all_to_all(
             g_send.reshape(group_count, capacity, ff_full),

time: 685 us -> 686 us (level)
  no operation moved by 1% of the time
where the time goes in v1:
time: 686 us; the launch traced here: 676 us
  other arithmetic  387 us (56%)
  local copies, waits for them, and re-layouts  93.3 us (14%)
  matrix products  90.7 us (13%)
  blocking collectives  79 us (12%)
  between operations  15.7 us (2%)
  starting transfers between devices  10.5 us (2%)
    another operation x18, other arithmetic, invert_blocks(): lower = jnp.linalg.cholesky(blocks)  203 us
    another operation x7, other arithmetic, invert_blocks(): jax.scipy.linalg.cho_solve((factor, True), identity)  124 us
    unnamed x3, other arithmetic  45.2 us
    psum x1, blocking collectives, local(): norm_total = lax.psum(jnp.sum(precond * precond), ('expert', 'shard'))  41.2 us
    dot_general x1, matrix products, local(): jnp.einsum('dcj,cjk->dck', left_done.reshape(width, ff_dev // BLK, BLK),...  36.8 us
    dot_general x1, matrix products, local(): jnp.einsum('bij,bjf->bif', lax.all_gather(inv_a, 'shard', axis=0, tiled=T...  22.9 us
    unnamed x1, blocking collectives  22.1 us
    reshape x1, local copies, waits for them, and re-layouts, local(): left_done.reshape(width, ff_dev // BLK, BLK)  20.4 us
  transfers between devices with their start and end apart: 5, of which 0 were waited for; matrix products, arithmetic and copies ran while one was open for 69% of the time, Pallas kernels for 0%

profile of v1, /device:TPU:0, one launch (start us, length us, event | category | flops | bytes accessed | tf_op | source)
XLA Modules:
  0.0 676.3 jit_solution(18162337235696644007)
XLA Ops:
  9.4 15.7 %all_to_all.49 = bf16[4,1,20,4096]{3,2,1,0:T(8,128)(2,1)S(1)} all-to-all(bf16[4,1,20,4096]{3,2,1,0:T(8,128)(2,1)S(1)} %pad_maximum_fusion), channel_id=1, replica_groups=mesh['expert'=4,'shard'=8] {'expert'}, dimensions={0} | all-to-all | bytes 1310720 | tf_op jit(solution)/shard_map/all_to_all | solution.py:11
  41.7 22.1 %all-reduce.2 = bf16[640]{0:T(1024)(128)(2,1)S(1)} all-reduce(bf16[640]{0:T(1024)(128)(2,1)S(1)} %dynamic-update-slice.22), channel_id=1, replica_groups=mesh['expert'=4,'shard'=8] {'shard'}, use_global_device_ids=true, to_apply=%add.2 | all-reduce | flops 640 | bytes 2560
  64.9 6.8 %copy.134 = bf16[1,80,8192]{1,0,2:T(2,128)(2,1)} copy(bf16[1,80,8192]{2,1,0:T(8,128)(2,1)S(1)} %all_to_all.36) | data formatting | bytes 2621440 | tf_op jit(solution)/shard_map/all_to_all | solution.py:62
  72.2 45.2 %reduce.30 = bf16[8192,80]{1,0:T(8,128)(2,1)S(1)} reduce(bf16[8192,1,80]{2,1,0:T(2,128)(2,1)} %bitcast.122, bf16[]{:T(256)} %broadcast.357), dimensions={1}, to_apply=%bitcast.79.reduce_sub_computation | reduce | bytes 2621442
  129.3 23.5 %custom-call.44 = f32[2,128,128]{2,1,0:T(8,128)S(1)} custom-call(f32[2,128,128]{2,1,0:T(8,128)S(1)} %cholesky.241), custom_call_target="Cholesky" | custom-call | tf_op jit(solution)/shard_map/jit(cholesky)/cholesky | solution.py:16
  153.5 19.7 %custom-call.45 = f32[2,1,128,128]{2,3,1,0:T(8,128)S(1)} custom-call(f32[2,1,128,128]{3,2,1,0:T(8,128)S(1)} %select_bitcast_fusion.1), custom_call_target="InvertDiagBlocksLowerTriangular" | custom-call | tf_op jit(solution)/shard_map/jit(cholesky)/cholesky | solution.py:16
  173.9 23.5 %custom-call.46 = f32[2,128,128]{2,1,0:T(8,128)S(1)} custom-call(f32[2,128,128]{2,1,0:T(8,128)S(1)} %convolution_subtract_fusion.5), custom_call_target="Cholesky" | custom-call | tf_op jit(solution)/shard_map/jit(cholesky)/cholesky | solution.py:16
  199.3 5.3 while.3
  204.6 40.3 %custom-call.47 = f32[2,2,128,128]{2,3,1,0:T(8,128)S(1)} custom-call(f32[2,2,128,128]{3,2,1,0:T(8,128)} %bitcast.133), custom_call_target="InvertDiagBlocksLowerTriangular" | custom-call | tf_op jit(solution)/shard_map/vmap(jit(_cho_solve))/triangular_solve | solution.py:18
  249.1 5.7 reshape.243
  254.9 8.3 %copy.135 = bf16[1,80,8192]{2,1,0:T(8,128)(2,1)S(1)} copy(bf16[1,80,8192]{1,0,2:T(2,128)(2,1)} %bitcast.123) | data formatting | bytes 2621440 | tf_op jit(solution)/shard_map/all_to_all | solution.py:81
  273.6 47.3 %custom-call.40 = f32[4,128,128]{2,1,0:T(8,128)S(1)} custom-call(f32[4,128,128]{2,1,0:T(8,128)S(1)} %cholesky.238), custom_call_target="Cholesky" | custom-call | tf_op jit(solution)/shard_map/jit(cholesky)/cholesky | solution.py:16
  321.1 39.9 %custom-call.41 = f32[4,1,128,128]{2,3,1,0:T(8,128)} custom-call(f32[4,1,128,128]{3,2,1,0:T(8,128)S(1)} %select_bitcast_fusion), custom_call_target="InvertDiagBlocksLowerTriangular" | custom-call | tf_op jit(solution)/shard_map/jit(cholesky)/cholesky | solution.py:16
  364.8 47.7 %custom-call.42 = f32[4,128,128]{2,1,0:T(8,128)S(1)} custom-call(f32[4,128,128]{2,1,0:T(8,128)} %convolution_subtract_fusion.4), custom_call_target="Cholesky" | custom-call | tf_op jit(solution)/shard_map/jit(cholesky)/cholesky | solution.py:16
  414.9 5.3 while.2
  420.3 79.6 %custom-call.43 = f32[4,2,128,128]{2,3,1,0:T(8,128)S(1)} custom-call(f32[4,2,128,128]{3,2,1,0:T(8,128)} %bitcast.132), custom_call_target="InvertDiagBlocksLowerTriangular" | custom-call | tf_op jit(solution)/shard_map/vmap(jit(_cho_solve))/triangular_solve | solution.py:18
  505.5 7.8 %copy.157 = bf16[4096,640]{1,0:T(8,128)(2,1)} copy(bf16[4096,640]{0,1:T(8,128)(2,1)} %bitcast.124) | data formatting | bytes 10485760 | tf_op jit(solution)/shard_map/dot_general | solution.py:85
  513.3 12.7 %fusion.41 = f32[16,256,1024]{2,1,0:T(8,128)} fusion(bf16[16,256,640]{2,1,0:T(8,128)(2,1)} %bitcast.125, bf16[640,1024,1]{1,0,2:T(8,128)(2,1)S(1)} %bitcast.126), kind=kOutput, calls=%fused_computation.103 | convolution fusion | flops 5368709120 | bytes 23330816 | tf_op jit(solution)/shard_map/dot_general | solution.py:85
  526.0 22.9 %fusion.42 = f32[16,256,1024]{2,1,0:T(8,128)} fusion(f32[16,256,256]{2,1,0:T(8,128)} %all-gather.5.cloned.1.call-done, f32[16,256,1024]{2,1,0:T(8,128)} %fusion.41), kind=kOutput, calls=%fused_computation.104 | convolution fusion | flops 12884901888 | bytes 37748736 | tf_op jit(solution)/shard_map/bij,bjf->bif/dot_general | solution.py:96
  548.9 20.4 %reshape.190 = f32[4096,4,256]{2,1,0:T(4,128)} reshape(f32[16,256,1024]{2,1,0:T(8,128)} %fusion.42) | data formatting | bytes 33554432 | tf_op jit(solution)/shard_map/reshape | solution.py:103
  569.3 36.8 %multiply_reduce_fusion = (f32[]{:T(128)}, f32[4,256,4096]{2,1,0:T(8,128)}) fusion(f32[4096,4,256]{2,1,0:T(4,128)} %reshape.190, f32[4,128,256]{2,1,0:T(8,128)S(1)} %fusion.14, f32[4,128,256]{2,1,0:T(8,128)S(1)} %fusion.13), kind=kOutput, calls=%fused_computation.7 | convolution fusion | flops 12893552640 | bytes 34603012 | tf_op jit(solution)/shard_map/dcj,cjk->dck/dot_general | solution.py:102
  606.1 41.2 %psum.7 = f32[]{:T(128)} all-reduce(f32[]{:T(128)} %get-tuple-element.57), channel_id=1, replica_groups=mesh['expert'=4,'shard'=8] {'expert','shard'}, use_global_device_ids=true, to_apply=%region_14.15 | all-reduce | flops 1 | bytes 8 | tf_op jit(solution)/shard_map/psum | solution.py:105
  647.9 9.1 %multiply_convert_fusion = bf16[4,256,4096]{2,1,0:T(8,128)(2,1)} fusion(f32[4,256,4096]{2,1,0:T(8,128)} %get-tuple-element.58, f32[]{:T(128)S(6)} %rsqrt.3), kind=kLoop, calls=%fused_computation.6 | loop fusion | flops 8388608 | bytes 25165828 | tf_op jit(solution)/shard_map/convert_element_type | solution.py:107
  657.1 12.0 %copy.161 = bf16[1,4096,1024]{2,1,0:T(8,128)(2,1)} copy(bf16[1,4096,1024]{1,2,0:T(8,128)(2,1)} %bitcast.121) | data formatting | bytes 16777216 | tf_op jit(solution)/shard_map/convert_element_type | solution.py:107
  (130 shorter events, 72.5 us)
Async XLA Ops:
  6.5 2.2 copy-start
  6.5 119.3 %all-gather.3.cloned.1.call-start = ((), (), s32[]{:S(2)}) async-start(), calls=%async_computation.4 | async-start | bytes 5898240 | tf_op jit(solution)/shard_map/all_gather | solution.py:78
  26.0 7.4 %copy-start.10 = (u32[32]{0:T(128)S(1)}, u32[32]{0:T(128)}, u32[]{:S(2)}) copy-start(u32[32]{0:T(128)} %constant.263) | copy-start | bytes 388
  26.9 7.9 %all-to-all-start.2 = ((bf16[4,1,20]{2,1,0:T(2,128)(2,1)}), bf16[4,1,20]{2,1,0:T(2,128)(2,1)S(1)}, u32[]{:S(2)}, u32[]{:S(2)}) async-start(bf16[4,1,20]{2,1,0:T(2,128)(2,1)} %all_to_all.44), calls=%async_computation.2 | async-start | bytes 4096 | tf_op jit(solution)/shard_map/all_to_all | solution.py:69
  31.5 7.3 %copy-start.8 = (s32[1,16]{1,0:T(1,128)S(1)}, s32[1,16]{1,0:T(1,128)}, u32[]{:S(2)}) copy-start(s32[1,16]{1,0:T(1,128)} %param.8) | copy-start | bytes 196
  34.8 29.8 %all-to-all-start = ((bf16[4,20,8192]{2,1,0:T(8,128)(2,1)}), bf16[4,20,8192]{2,1,0:T(8,128)(2,1)S(1)}, u32[]{:S(2)}, u32[]{:S(2)}) async-start(bf16[4,20,8192]{2,1,0:T(8,128)(2,1)} %reshape.185), calls=%async_computation | async-start | bytes 3145728 | tf_op jit(solution)/shard_map/all_to_all | solution.py:62
  122.0 127.1 %all-to-all-start.1 = ((bf16[8,2,40960]{2,1,0:T(2,128)(2,1)}), bf16[8,2,40960]{2,1,0:T(2,128)(2,1)S(1)}, u32[]{:S(2)}, u32[]{:S(2)}) async-start(bf16[8,2,40960]{2,1,0:T(2,128)(2,1)} %reshape.242), calls=%async_computation.1 | async-start | bytes 2621440 | tf_op jit(solution)/shard_map/all_to_all | solution.py:81
  125.6 400.4 %all-gather.5.cloned.1.call-start = ((), (), s32[]{:S(2)}) async-start(), calls=%async_computation.5 | async-start | bytes 4718592 | tf_op jit(solution)/shard_map/all_gather | solution.py:98
  197.6 51.5 %copy-start.9 = (s32[1,4]{1,0:T(1,128)S(1)}, s32[1,4]{1,0:T(1,128)}, u32[]{:S(2)}) copy-start(s32[1,4]{1,0:T(1,128)} %param.9) | copy-start | bytes 52
  269.8 51.2 %copy-start.7 = (pred[128,128]{1,0:T(8,128)(4,1)S(1)}, pred[128,128]{1,0:T(8,128)(4,1)}, u32[]{:S(2)}) copy-start(pred[128,128]{1,0:T(8,128)(4,1)} %iota_compare_fusion.3) | copy-start | bytes 49156
  271.1 142.4 %copy-start.6 = (pred[256,256]{1,0:T(8,128)(4,1)S(1)}, pred[256,256]{1,0:T(8,128)(4,1)}, u32[]{:S(2)}) copy-start(pred[256,256]{1,0:T(8,128)(4,1)} %iota_compare_fusion.2) | copy-start | bytes 196612
  272.6 1.0 copy-start.3
  361.0 139.5 %copy-start.5 = (f32[128,256]{1,0:T(8,128)S(1)}, f32[128,256]{1,0:T(8,128)}, u32[]{:S(2)}) copy-start(f32[128,256]{1,0:T(8,128)} %get-tuple-element.50) | copy-start | bytes 393220
  412.6 1.0 copy-start.2
  499.9 1.2 copy-start.4
  657.1 12.0 %copy-start.1 = (bf16[32,4096]{1,0:T(8,128)(2,1)S(1)}, bf16[32,4096]{1,0:T(8,128)(2,1)}, u32[]{:S(2)}) copy-start(bf16[32,4096]{1,0:T(8,128)(2,1)} %param.5) | copy-start | bytes 786436
Sparse Core Ops, SparseCore 0:
  26.2 86.4 all-gather.2
  249.2 74.5 all-gather.4
